TPU v7x, 32 devices: a whole 2x2x4 slice. The times are simulated.
32 devices in a mesh: groups: 2 (over y), sess: 4 (over z), inner: 2 (over x), rep: 2 (over core).
Axes of the slice: x: 2, y: 2, z: 4, core: 2. Of those that a mesh axis runs over, the one named last changes fastest.
Arguments:
- thinker_rows: bfloat16 [4096, 3584], P(('groups', 'sess', 'rep'), 'inner'), parts along dimension 0, may hold values from -6 to 6
- row_session: int32 [4096, 1], P(('groups', 'sess', 'rep')), parts along dimension 0, may hold values from 0 to 31; in each aligned block of 256 rows (0 to 255, 256 to 511, ...) at most 12 rows name the same one
- speaker_of: int32 [64], P('groups'), parts along dimension 0, may hold values from 0 to 7
- prompt_slot: int32 [16], P('groups'), parts along dimension 0, may hold values from 0 to 7, each once
- prompt_cache: bfloat16 [16, 1024, 1024], P(('groups', 'sess'), ('inner', 'rep')), parts along dimension 0, may hold values from -64 to 64
- proj_weight: bfloat16 [3584, 896], P('inner'), may hold values from -0.09375 to 0.09375
- attn_gain: bfloat16 [896], replicated, may hold values from 0.5 to 1.5
- q_weight: bfloat16 [896, 1536], replicated, may hold values from -0.1875 to 0.1875
- k_weight: bfloat16 [896, 512], replicated, may hold values from -0.625 to 0.625
- v_weight: bfloat16 [896, 512], replicated, may hold values from -0.1875 to 0.1875
- o_weight: bfloat16 [1536, 896], replicated, may hold values from -0.15625 to 0.15625
Outputs:
- voice_states: bfloat16 [64, 96, 896], P(('groups', 'sess', 'inner', 'rep')), parts along dimension 0
There are 2 independent parts, one for each index of `groups`. A program takes and returns all parts, laid end to end along the dimension named above; an argument that names none is the same for every part. Nothing has to cross between parts.
Inputs may be any that keep to these rules, and one draw needn't show every extreme that they name: `row_session`: column 0 names the session of the row. Within each block of 256 rows (rows b * 256 to (b + 1) * 256 - 1, the rows of one index of sess+rep) no session is named by more than 12 rows, a bound that some block reaches; every session is named by some row. `prompt_slot`: each slot holds exactly one speaker's prompt.
All inputs are finite; a program needn't handle non-finite values.
Results may differ from a plain program's by a relative error of at most 0.0071.
Values may be sent and summed in bfloat16 or wider, within the bound.
No kernel may reach another device: no remote copies, remote signals or barrier semaphores. Data moves between devices by JAX's collectives and lax.ppermute only.
A program may use at most 128 MiB of HBM per device.

v0:
```python
import jax
import jax.numpy as jnp
from jax import lax
from jax.sharding import PartitionSpec as P

H = 12
KVH = 4
HD = 128
PROMPT = 1024
SLOTS = 96
EPSILON = 1e-06
ROPE_BASE = 1000000.0


def rms_scale(states, gain):
    widened = states.astype(jnp.float32)
    factor = lax.rsqrt(jnp.mean(widened * widened, axis=-1, keepdims=True) + EPSILON)
    return (widened * factor * gain.astype(jnp.float32)).astype(jnp.bfloat16)


def rope_tables(slot_total):
    half_width = HD // 2
    inverse = ROPE_BASE ** (-(jnp.arange(half_width, dtype=jnp.float32) * 2.0) / HD)
    angles = (PROMPT + jnp.arange(slot_total)).astype(jnp.float32)[:, None] * inverse[None, :]
    cosine = jnp.concatenate([jnp.cos(angles), jnp.cos(angles)], axis=1)[:, None, :]
    sine_table = jnp.concatenate([jnp.sin(angles), jnp.sin(angles)], axis=1)[:, None, :]
    return (cosine, sine_table)


def rotate(vectors, cosine, sine_table):
    half_width = vectors.shape[-1] // 2
    turned = jnp.concatenate([-vectors[..., half_width:], vectors[..., :half_width]], axis=-1)
    return vectors * cosine + turned * sine_table


def attend(states, lengths, prompts, attn_gain, q_weight, k_weight, v_weight, o_weight):
    session_total, slot_total, model_width = states.shape
    flat_rows = states.reshape(session_total * slot_total, model_width)
    normed = rms_scale(flat_rows, attn_gain)
    cosine, sine_table = rope_tables(slot_total)
    query = rotate(
        jnp.dot(normed, q_weight, preferred_element_type=jnp.float32).reshape(
            session_total, slot_total, H, HD
        ),
        cosine,
        sine_table,
    ).astype(jnp.bfloat16)
    own_keys = rotate(
        jnp.dot(normed, k_weight, preferred_element_type=jnp.float32).reshape(
            session_total, slot_total, KVH, HD
        ),
        cosine,
        sine_table,
    ).astype(jnp.bfloat16)
    own_values = (
        jnp.dot(normed, v_weight, preferred_element_type=jnp.float32)
        .reshape(session_total, slot_total, KVH, HD)
        .astype(jnp.bfloat16)
    )
    prompt_keys = prompts[:, :, : KVH * HD].reshape(session_total, PROMPT, KVH, HD)
    prompt_values = prompts[:, :, KVH * HD :].reshape(session_total, PROMPT, KVH, HD)
    all_keys = jnp.concatenate([prompt_keys, own_keys], axis=1)
    all_values = jnp.concatenate([prompt_values, own_values], axis=1)
    key_place = jnp.arange(PROMPT + slot_total) - PROMPT
    query_place = jnp.arange(slot_total)
    allowed = (key_place[None, None, :] < 0) | (
        key_place[None, None, :] <= query_place[None, :, None]
    ) & (key_place[None, None, :] < lengths[:, None, None])
    per_group = H // KVH
    outputs = []
    for kv_head in range(KVH):
        query_group = query[:, :, kv_head * per_group : (kv_head + 1) * per_group]
        scores = jnp.einsum(
            "cqhd,ckd->chqk",
            query_group,
            all_keys[:, :, kv_head],
            preferred_element_type=jnp.float32,
        ) * HD ** (-0.5)
        scores = jnp.where(allowed[:, None], scores, -1e30)
        highest = jnp.max(scores, axis=-1, keepdims=True)
        powers = jnp.exp(scores - highest)
        weights = (powers / jnp.sum(powers, axis=-1, keepdims=True)).astype(jnp.bfloat16)
        outputs.append(
            jnp.einsum(
                "chqk,ckd->cqhd",
                weights,
                all_values[:, :, kv_head],
                preferred_element_type=jnp.float32,
            )
        )
    attended = (
        jnp.concatenate(outputs, axis=2)
        .reshape(session_total * slot_total, H * HD)
        .astype(jnp.bfloat16)
    )
    return flat_rows.astype(jnp.float32) + jnp.dot(
        attended, o_weight, preferred_element_type=jnp.float32
    )


def body(
    thinker_rows,
    row_session,
    speaker_of,
    prompt_slot,
    prompt_cache,
    proj_weight,
    attn_gain,
    q_weight,
    k_weight,
    v_weight,
    o_weight,
):
    sess_count = lax.axis_size("sess")
    inner_count = lax.axis_size("inner")
    rep_count = lax.axis_size("rep")
    owner_count = sess_count * rep_count
    session_all = speaker_of.shape[0]
    per_device = session_all // (owner_count * inner_count)
    per_owner = per_device * inner_count
    slot_cap = SLOTS // owner_count
    inner_place = lax.axis_index("inner")
    shard_place = lax.axis_index("sess")
    row_owner = row_session[:, 0]
    device_of = row_owner // per_device
    target = (
        (device_of // (inner_count * rep_count) * rep_count + device_of % rep_count) * per_owner
        + device_of // rep_count % inner_count * per_device
        + row_owner % per_device
    )
    row_order = jnp.arange(row_owner.shape[0])
    earlier = jnp.sum(
        (
            (row_owner[:, None] == row_owner[None, :]) & (row_order[None, :] < row_order[:, None])
        ).astype(jnp.int32),
        axis=1,
    )
    slot_place = target * slot_cap + earlier
    counts = jnp.sum(
        (target[:, None] == jnp.arange(owner_count * per_owner)[None, :]).astype(jnp.int32), axis=0
    ).reshape(owner_count, per_owner)
    partial_sum = jnp.dot(thinker_rows, proj_weight, preferred_element_type=jnp.float32)
    own_columns = lax.psum_scatter(partial_sum, "inner", scatter_dimension=1, tiled=True).astype(
        jnp.bfloat16
    )
    buffer = (
        jnp.zeros((owner_count * per_owner * slot_cap, own_columns.shape[1]), own_columns.dtype)
        .at[slot_place]
        .set(own_columns)
    )
    arrived = lax.all_to_all(
        buffer.reshape(owner_count, per_owner * slot_cap, own_columns.shape[1]),
        ("sess", "rep"),
        split_axis=0,
        concat_axis=0,
        tiled=True,
    )
    counts_in = lax.all_to_all(counts, ("sess", "rep"), split_axis=0, concat_axis=0, tiled=True)
    arrived_rows = arrived.reshape(owner_count, per_owner, slot_cap, arrived.shape[2])
    regrouped = lax.all_to_all(arrived_rows, "inner", split_axis=1, concat_axis=3, tiled=True)
    projected = jnp.transpose(regrouped, (1, 0, 2, 3)).reshape(
        per_device, owner_count * slot_cap, regrouped.shape[3]
    )
    own_counts = lax.dynamic_slice_in_dim(counts_in, inner_place * per_device, per_device, 1)
    offsets = jnp.cumsum(own_counts, axis=0) - own_counts
    lengths = jnp.sum(own_counts, axis=0)
    within = jnp.arange(slot_cap)
    position = jnp.transpose(offsets)[:, :, None] + within[None, None, :]
    live_slot = within[None, None, :] < jnp.transpose(own_counts)[:, :, None]
    position = jnp.where(live_slot, position, SLOTS).reshape(per_device, owner_count * slot_cap)
    session_rows = jnp.broadcast_to(jnp.arange(per_device)[:, None], position.shape)
    compact = (
        jnp.zeros((per_device, SLOTS, projected.shape[2]), jnp.bfloat16)
        .at[session_rows, position]
        .set(projected, mode="drop")
    )
    shard_sessions = per_device * inner_count * rep_count
    wanted_speaker = lax.dynamic_slice_in_dim(
        speaker_of, shard_place * shard_sessions, shard_sessions
    )
    speaker_table = jnp.arange(prompt_slot.shape[0])
    wanted_slot = jnp.sum(
        jnp.where(wanted_speaker[:, None] == speaker_table[None, :], prompt_slot[None, :], 0),
        axis=1,
    )
    piece = lax.all_gather(prompt_cache, "sess", axis=0, tiled=True)
    matching = (wanted_slot[:, None] == jnp.arange(piece.shape[0])[None, :]).astype(jnp.bfloat16)
    chosen = jnp.einsum("sp,ptc->stc", matching, piece, preferred_element_type=jnp.float32)
    prompts = lax.all_to_all(
        chosen.astype(jnp.bfloat16), ("inner", "rep"), split_axis=0, concat_axis=1, tiled=True
    )
    summed = attend(compact, lengths, prompts, attn_gain, q_weight, k_weight, v_weight, o_weight)
    live_rows = (jnp.arange(SLOTS)[None, :] < lengths[:, None]).reshape(-1, 1)
    return (
        jnp.where(live_rows, summed, 0.0)
        .astype(jnp.bfloat16)
        .reshape(per_device, SLOTS, summed.shape[1])
    )


def solution(mesh):
    in_specs = (
        P(("groups", "sess", "rep"), "inner"),
        P(("groups", "sess", "rep"), None),
        P("groups"),
        P("groups"),
        P(("groups", "sess"), ("inner", "rep"), None),
        P("inner", None),
        P(),
        P(),
        P(),
        P(),
        P(),
    )
    out_specs = P(("groups", "sess", "inner", "rep"), None, None)
    return jax.shard_map(body, mesh=mesh, in_specs=in_specs, out_specs=out_specs, check_vma=False)
```

profile of v0, /device:TPU:0, one launch (start us, length us, event | category | flops | bytes accessed | tf_op | source)
XLA Modules:
  0.0 214.4 jit_solution(5181493876565836849)
XLA Ops:
  7.4 1.9 copy-done
  9.3 3.5 %fusion.175 = f32[256,896]{0,1:T(8,128)} fusion(bf16[256,1792]{1,0:T(8,128)(2,1)} %param.11, bf16[1792,896]{1,0:T(8,128)(2,1)S(1)} %copy-done), kind=kOutput, calls=%fused_computation.189 | convolution fusion | flops 822083584 | bytes 5046272 | tf_op jit(solution)/shard_map/dot_general | solution.py:142
  12.8 0.5 all-gather.2.cloned.1.call-update
  13.7 0.7 all_to_all.35
  14.4 6.3 %all-to-all-start = ((s32[8,1,4]{2,1,0:T(1,128)}), s32[8,1,4]{2,1,0:T(1,128)S(1)}, u32[]{:S(2)}, u32[]{:S(2)}) async-start(s32[8,1,4]{2,1,0:T(1,128)} %bitcast.1), calls=%async_computation | async-start | bytes 8192 | tf_op jit(solution)/shard_map/all_to_all | solution.py:158
  20.7 4.9 %copy.90 = bf16[896,1536]{0,1:T(8,128)(2,1)} copy(bf16[896,1536]{1,0:T(8,128)(2,1)} %param.18) | data formatting | bytes 5505024 | tf_op args[7]
  25.7 0.6 copy.102
  26.9 0.7 pad_maximum_fusion.3
  27.7 1.3 copy.101
  29.3 5.2 %reduce-scatter.2.cloned.1.call-done = f32[256,448]{0,1:T(8,128)} async-done(((f32[256,896]{0,1:T(8,128)}), f32[256,448]{0,1:T(8,128)}) %reduce-scatter.2.cloned.1.call-update) | async-done | bytes 458768 | tf_op jit(solution)/shard_map/reduce_scatter | solution.py:143
  34.5 1.0 convert_element_type.78
  35.7 2.2 %scatter_custom_fusion = bf16[384,448]{1,0:T(8,128)(2,1)} fusion(s32[256]{0:T(256)S(1)} %bitcast.200, bf16[256,448]{1,0:T(8,128)(2,1)S(1)} %copy.75, bf16[]{:T(256)} %constant.95.clone.1), kind=kCustom, calls=%fused_computation.98 | custom fusion | bytes 344066 | tf_op jit(solution)/shard_map/scatter | solution.py:149
  38.0 4.6 %all-to-all-start.1 = ((bf16[8,48,448]{2,1,0:T(8,128)(2,1)}), bf16[8,48,448]{2,1,0:T(8,128)(2,1)S(1)}, u32[]{:S(2)}, u32[]{:S(2)}) async-start(bf16[8,48,448]{2,1,0:T(8,128)(2,1)} %bitcast.8), calls=%async_computation.2 | async-start | bytes 786432 | tf_op jit(solution)/shard_map/all_to_all | solution.py:151
  43.1 0.6 lt.139
  43.7 24.4 %all-to-all-done.1 = bf16[8,48,448]{2,1,0:T(8,128)(2,1)S(1)} async-done(((bf16[8,48,448]{2,1,0:T(8,128)(2,1)}), bf16[8,48,448]{2,1,0:T(8,128)(2,1)S(1)}, u32[]{:S(2)}, u32[]{:S(2)}) %all-to-all-start.1) | async-done | bytes 344096 | tf_op jit(solution)/shard_map/all_to_all | solution.py:151
  68.1 1.0 copy.76
  69.1 3.5 %all-to-all-start.2 = ((bf16[8,4,12,448]{3,0,2,1:T(8,128)(2,1)}), bf16[8,4,12,448]{3,0,2,1:T(8,128)(2,1)S(1)}, u32[]{:S(2)}, u32[]{:S(2)}) async-start(bf16[8,4,12,448]{3,0,2,1:T(8,128)(2,1)} %bitcast.9), calls=%async_computation.3 | async-start | bytes 786432 | tf_op jit(solution)/shard_map/all_to_all | solution.py:160
  72.5 33.9 %all-gather.2.cloned.1.call-done = bf16[8,256,1024]{2,1,0:T(8,128)(2,1)} async-done(((bf16[2,256,1024]{2,1,0:T(8,128)(2,1)}), bf16[8,256,1024]{2,1,0:T(8,128)(2,1)}) %all-gather.2.cloned.1.call-update) | async-done | bytes 4194320 | tf_op jit(solution)/shard_map/all_gather | solution.py:186
  106.4 4.7 %fusion.22 = bf16[8,256,1024]{2,0,1:T(8,128)(2,1)S(1)} fusion(bf16[8,256,1024]{2,1,0:T(8,128)(2,1)} %all-gather.2.cloned.1.call-done, s32[8]{0:T(128)S(1)} %select_reduce_fusion), kind=kOutput, calls=%fused_computation.34 | convolution fusion | flops 35651648 | bytes 8388640 | tf_op jit(solution)/shard_map/sp,ptc->stc/dot_general | solution.py:188
  111.2 4.3 %copy.80 = bf16[8,256,1024]{2,1,0:T(8,128)(2,1)} copy(bf16[8,256,1024]{2,0,1:T(8,128)(2,1)S(1)} %fusion.22) | data formatting | bytes 8388608 | tf_op jit(solution)/shard_map/convert_element_type | solution.py:190
  115.4 5.0 %all-to-all-start.3 = ((bf16[8,256,1024]{2,1,0:T(8,128)(2,1)}), bf16[8,256,1024]{2,1,0:T(8,128)(2,1)}, u32[]{:S(2)}, u32[]{:S(2)}) async-start(bf16[8,256,1024]{2,1,0:T(8,128)(2,1)} %copy.80), calls=%async_computation.4 | async-start | bytes 8388608 | tf_op jit(solution)/shard_map/all_to_all | solution.py:189
  120.5 0.8 and_or_fusion
  122.3 13.1 %scatter_fusion = bf16[2,96,896]{2,1,0:T(8,128)(2,1)S(1)} fusion(bf16[2,96,896]{2,1,0:T(8,128)(2,1)S(1)} %broadcast_in_dim.55, s32[192]{0:T(256)S(1)} %reshape.305, bf16[192,896]{1,0:T(8,128)(2,1)S(1)} %reshape.307), kind=kCustom, calls=%fused_computation.1 | custom fusion | bytes 1033728 | tf_op jit(solution)/shard_map/scatter | solution.py:175
  135.5 0.5 fusion.115
  136.2 0.9 fusion.68
  137.1 1.2 convolution_convert_fusion
  138.3 1.1 fusion.113
  139.8 0.4 fusion.32
  140.3 28.3 %all-to-all-done.3 = bf16[8,256,1024]{2,1,0:T(8,128)(2,1)} async-done(((bf16[8,256,1024]{2,1,0:T(8,128)(2,1)}), bf16[8,256,1024]{2,1,0:T(8,128)(2,1)}, u32[]{:S(2)}, u32[]{:S(2)}) %all-to-all-start.3) | async-done | bytes 4194336 | tf_op jit(solution)/shard_map/all_to_all | solution.py:189
  168.5 2.6 %copy.81 = bf16[2,4,256,1024]{3,2,1,0:T(8,128)(2,1)S(1)} copy(bf16[2,4,256,1024]{3,2,0,1:T(8,128)(2,1)} %bitcast.16) | data formatting | bytes 8388608 | tf_op jit(solution)/shard_map/all_to_all | solution.py:189
  171.1 2.5 %fusion.154 = (bf16[2,1024,512]{2,1,0:T(8,128)(2,1)}, bf16[2,1024,512]{2,1,0:T(8,128)(2,1)}) fusion(bf16[2,1024,1024]{2,1,0:T(8,128)(2,1)S(1)} %bitcast.185), kind=kLoop, calls=%fused_computation.184 | loop fusion | bytes 8388608 | tf_op jit(solution)/shard_map/slice | solution.py:61
  173.6 3.0 %copy.86 = bf16[2,1024,512]{1,2,0:T(8,128)(2,1)S(1)} copy(bf16[2,1024,512]{2,1,0:T(8,128)(2,1)} %get-tuple-element.10) | data formatting | bytes 4194304 | tf_op jit(solution)/shard_map/slice | solution.py:60
  176.7 2.5 %copy.88 = bf16[2,1024,4,128]{3,1,0,2:T(8,128)(2,1)} copy(bf16[2,1024,4,128]{1,3,2,0:T(8,128)(2,1)S(1)} %bitcast.187) | data formatting | bytes 4194304 | tf_op jit(solution)/shard_map/reshape | solution.py:60
  179.2 3.8 %fusion.155 = (f32[2,3,96]{2,1,0:T(4,128)S(1)}, f32[2,3,96,1120]{3,2,1,0:T(8,128)}) fusion(pred[2,96,1120]{2,1,0:T(8,128)(4,1)S(1)} %copy-done.9, bf16[2,1024,4,128]{3,1,0,2:T(8,128)(2,1)} %copy.88, bf16[2,96,12,128]{3,1,2,0:T(8,128)(2,1)S(1)} %fusion.32, bf16[2,96,4,128]{3,1,2,0:T(8,128)(2,1)S(1)} %copy-done.10), kind=kOutput, calls=%fused_computation.185 | convolution fusion | flops 168879200 | bytes 5245184 | tf_op jit(solution)/shard_map/sub | solution.py:81
  183.0 2.6 %fusion.160 = (f32[2,3,96]{2,1,0:T(4,128)S(1)}, f32[2,3,96,1120]{3,2,1,0:T(8,128)}) fusion(pred[2,96,1120]{2,1,0:T(8,128)(4,1)S(1)} %copy-done.9, bf16[2,1024,4,128]{3,1,0,2:T(8,128)(2,1)S(1)} %copy-done.4, bf16[2,96,12,128]{3,1,2,0:T(8,128)(2,1)S(1)} %fusion.32, bf16[2,96,4,128]{3,1,2,0:T(8,128)(2,1)S(1)} %copy-done.10), kind=kOutput, calls=%fused_computation.186 | convolution fusion | flops 168879200 | bytes 5245184 | tf_op jit(solution)/shard_map/sub | solution.py:81
  185.7 2.6 %fusion.165 = (f32[2,3,96]{2,1,0:T(4,128)S(1)}, f32[2,3,96,1120]{3,2,1,0:T(8,128)}) fusion(pred[2,96,1120]{2,1,0:T(8,128)(4,1)S(1)} %copy-done.9, bf16[2,1024,4,128]{3,1,0,2:T(8,128)(2,1)S(1)} %copy-done.4, bf16[2,96,12,128]{3,1,2,0:T(8,128)(2,1)S(1)} %fusion.32, bf16[2,96,4,128]{3,1,2,0:T(8,128)(2,1)S(1)} %copy-done.10), kind=kOutput, calls=%fused_computation.187 | convolution fusion | flops 168879200 | bytes 5245184 | tf_op jit(solution)/shard_map/sub | solution.py:81
  188.3 2.7 %fusion.170 = (f32[2,3,96]{2,1,0:T(4,128)S(1)}, f32[2,3,96,1120]{3,2,1,0:T(8,128)}) fusion(pred[2,96,1120]{2,1,0:T(8,128)(4,1)S(1)} %copy-done.9, bf16[2,1024,4,128]{3,1,0,2:T(8,128)(2,1)S(1)} %copy-done.4, bf16[2,96,12,128]{3,1,2,0:T(8,128)(2,1)S(1)} %fusion.32, bf16[2,96,4,128]{3,1,2,0:T(8,128)(2,1)S(1)} %copy-done.10), kind=kOutput, calls=%fused_computation.188 | convolution fusion | flops 168879200 | bytes 5245184 | tf_op jit(solution)/shard_map/sub | solution.py:81
  190.9 3.0 %copy.82 = bf16[2,1024,512]{1,2,0:T(8,128)(2,1)S(1)} copy(bf16[2,1024,512]{2,1,0:T(8,128)(2,1)} %get-tuple-element.9) | data formatting | bytes 4194304 | tf_op jit(solution)/shard_map/slice | solution.py:61
  193.9 2.9 %copy.84 = bf16[2,1024,4,128]{3,1,0,2:T(8,128)(2,1)} copy(bf16[2,1024,4,128]{1,3,2,0:T(8,128)(2,1)S(1)} %bitcast.188) | data formatting | bytes 4194304 | tf_op jit(solution)/shard_map/reshape | solution.py:61
  196.8 2.6 %fusion.40 = bf16[2,96,3,128]{3,1,2,0:T(8,128)(2,1)S(1)} fusion(f32[2,3,96,1120]{3,2,1,0:T(8,128)} %get-tuple-element.18, f32[2,3,96]{2,1,0:T(4,128)S(1)} %get-tuple-element.17, bf16[2,1024,4,128]{3,1,0,2:T(8,128)(2,1)} %copy.84, bf16[2,96,4,128]{3,1,2,0:T(8,128)(2,1)S(1)} %copy-done.17), kind=kOutput, calls=%fused_computation.64 | convolution fusion | flops 167661568 | bytes 5024000 | tf_op jit(solution)/shard_map/chqk,ckd->cqhd/dot_general | solution.py:84
  199.4 0.7 copy-done.20
  200.1 0.6 fusion.39
  200.7 1.2 copy-done.19
  201.9 0.6 fusion.38
  202.5 1.2 copy-done.18
  203.6 0.6 fusion.37
  204.6 0.8 copy-done.13
  205.4 1.5 fusion.30
  (80 shorter events, 4.2 us)
Async XLA Ops:
  7.4 1.9 copy-start
  7.4 6.0 %copy-start.11 = (s32[256,1]{0,1:T(1,128)S(1)}, s32[256,1]{0,1:T(1,128)}, u32[]{:S(2)}) copy-start(s32[256,1]{0,1:T(1,128)} %param.12) | copy-start | bytes 3076
  7.4 27.1 %reduce-scatter.2.cloned.1.call-start = ((), (), s32[]{:S(2)}) async-start(), calls=%async_computation.5 | async-start | bytes 1376256 | tf_op jit(solution)/shard_map/reduce_scatter | solution.py:143
  12.8 93.7 %all-gather.2.cloned.1.call-start = ((), (), s32[]{:S(2)}) async-start(), calls=%async_computation.6 | async-start | bytes 5242880 | tf_op jit(solution)/shard_map/all_gather | solution.py:186
  14.4 14.6 %all-to-all-start = ((s32[8,1,4]{2,1,0:T(1,128)}), s32[8,1,4]{2,1,0:T(1,128)S(1)}, u32[]{:S(2)}, u32[]{:S(2)}) async-start(s32[8,1,4]{2,1,0:T(1,128)} %bitcast.1), calls=%async_computation | async-start | bytes 8192 | tf_op jit(solution)/shard_map/all_to_all | solution.py:158
  20.7 5.0 %copy-start.12 = (bf16[896]{0:T(1024)(128)(2,1)S(1)}, bf16[896]{0:T(1024)(128)(2,1)}, u32[]{:S(2)}) copy-start(bf16[896]{0:T(1024)(128)(2,1)} %param.17) | copy-start | bytes 5380
  20.7 5.0 %copy-start.5 = (bf16[896,512]{1,0:T(8,128)(2,1)S(1)}, bf16[896,512]{1,0:T(8,128)(2,1)}, u32[]{:S(2)}) copy-start(bf16[896,512]{1,0:T(8,128)(2,1)} %param.19) | copy-start | bytes 2752516
  20.7 5.6 %copy-start.14 = (s32[32]{0:T(128)S(1)}, s32[32]{0:T(128)}, u32[]{:S(2)}) copy-start(s32[32]{0:T(128)} %param.13) | copy-start | bytes 388
  20.7 5.7 %copy-start.15 = (s32[8]{0:T(128)S(1)}, s32[8]{0:T(128)}, u32[]{:S(2)}) copy-start(s32[8]{0:T(128)} %param.14) | copy-start | bytes 100
  25.6 2.1 copy-start.6
  38.0 30.1 %all-to-all-start.1 = ((bf16[8,48,448]{2,1,0:T(8,128)(2,1)}), bf16[8,48,448]{2,1,0:T(8,128)(2,1)S(1)}, u32[]{:S(2)}, u32[]{:S(2)}) async-start(bf16[8,48,448]{2,1,0:T(8,128)(2,1)} %bitcast.8), calls=%async_computation.2 | async-start | bytes 786432 | tf_op jit(solution)/shard_map/all_to_all | solution.py:151
  69.1 46.4 %all-to-all-start.2 = ((bf16[8,4,12,448]{3,0,2,1:T(8,128)(2,1)}), bf16[8,4,12,448]{3,0,2,1:T(8,128)(2,1)S(1)}, u32[]{:S(2)}, u32[]{:S(2)}) async-start(bf16[8,4,12,448]{3,0,2,1:T(8,128)(2,1)} %bitcast.9), calls=%async_computation.3 | async-start | bytes 786432 | tf_op jit(solution)/shard_map/all_to_all | solution.py:160
  115.4 53.1 %all-to-all-start.3 = ((bf16[8,256,1024]{2,1,0:T(8,128)(2,1)}), bf16[8,256,1024]{2,1,0:T(8,128)(2,1)}, u32[]{:S(2)}, u32[]{:S(2)}) async-start(bf16[8,256,1024]{2,1,0:T(8,128)(2,1)} %copy.80), calls=%async_computation.4 | async-start | bytes 8388608 | tf_op jit(solution)/shard_map/all_to_all | solution.py:189
  135.3 0.9 copy-start.8
  135.5 1.6 copy-start.7
  136.0 2.2 %copy-start.2 = (bf16[896,1536]{0,1:T(8,128)(2,1)S(1)}, bf16[896,1536]{0,1:T(8,128)(2,1)}, u32[]{:S(2)}) copy-start(bf16[896,1536]{0,1:T(8,128)(2,1)} %copy.90) | copy-start | bytes 8257540
  176.6 2.6 %copy-start.9 = (pred[2,96,1120]{2,1,0:T(8,128)(4,1)S(1)}, pred[2,96,1120]{2,1,0:T(8,128)(4,1)}, u32[]{:S(2)}) copy-start(pred[2,96,1120]{2,1,0:T(8,128)(4,1)} %and_or_fusion) | copy-start | bytes 645124
  176.6 2.6 %copy-start.10 = (bf16[2,96,4,128]{3,1,2,0:T(8,128)(2,1)S(1)}, bf16[2,96,4,128]{3,1,2,0:T(8,128)(2,1)}, u32[]{:S(2)}) copy-start(bf16[2,96,4,128]{3,1,2,0:T(8,128)(2,1)} %fusion.68) | copy-start | bytes 589828
  179.2 3.8 %copy-start.4 = (bf16[2,1024,4,128]{3,1,0,2:T(8,128)(2,1)S(1)}, bf16[2,1024,4,128]{3,1,0,2:T(8,128)(2,1)}, u32[]{:S(2)}) copy-start(bf16[2,1024,4,128]{3,1,0,2:T(8,128)(2,1)} %copy.88) | copy-start | bytes 6291460
  193.9 2.9 %copy-start.17 = (bf16[2,96,4,128]{3,1,2,0:T(8,128)(2,1)S(1)}, bf16[2,96,4,128]{3,1,2,0:T(8,128)(2,1)}, u32[]{:S(2)}) copy-start(bf16[2,96,4,128]{3,1,2,0:T(8,128)(2,1)} %convolution_convert_fusion) | copy-start | bytes 589828
  196.8 2.6 %copy-start.3 = (bf16[2,1024,4,128]{3,1,0,2:T(8,128)(2,1)S(1)}, bf16[2,1024,4,128]{3,1,0,2:T(8,128)(2,1)}, u32[]{:S(2)}) copy-start(bf16[2,1024,4,128]{3,1,0,2:T(8,128)(2,1)} %copy.84) | copy-start | bytes 6291460
  196.8 3.3 %copy-start.20 = (f32[2,3,96,1120]{3,2,1,0:T(8,128)S(1)}, f32[2,3,96,1120]{3,2,1,0:T(8,128)}, u32[]{:S(2)}) copy-start(f32[2,3,96,1120]{3,2,1,0:T(8,128)} %get-tuple-element.20) | copy-start | bytes 7741444
  200.1 1.7 copy-start.19
  201.9 1.7 copy-start.18
  203.6 1.8 copy-start.13
  204.2 1.2 copy-start.16
  204.6 2.4 %copy-start.1 = (bf16[1792,896]{1,0:T(8,128)(2,1)S(1)}, bf16[1792,896]{1,0:T(8,128)(2,1)}, u32[]{:S(2)}) copy-start(bf16[1792,896]{1,0:T(8,128)(2,1)} %param.16) | copy-start | bytes 9633796
Sparse Core Ops, SparseCore 0:
  12.9 21.5 reduce-scatter.1
Sparse Core Ops, SparseCore 1:
  14.8 91.6 all-gather.1
where the time goes:
time: 215 us; the launch traced here: 214 us
  waiting for transfers between devices  92.3 us (43%)
  local copies, waits for them, and re-layouts  52.8 us (25%)
  matrix products  28.5 us (13%)
  starting transfers between devices  19.5 us (9%)
  between operations  15.2 us (7%)
  other arithmetic  6.03 us (3%)
    all_gather x1, waiting for transfers between devices, body(): piece = lax.all_gather(prompt_cache, 'sess', axis=0, tiled=True)  33.9 us
    all_to_all x1, waiting for transfers between devices, body(): lax.all_to_all(chosen.astype(jnp.bfloat16), ('inner', 'rep'), split_axis=...  28.3 us
    all_to_all x1, waiting for transfers between devices, body(): lax.all_to_all(buffer.reshape(owner_count, per_owner * slot_cap, own_colu...  24.4 us
    scatter x1, local copies, waits for them, and re-layouts, body(): compact = jnp.zeros((per_device, SLOTS, projected.shape[2]), jnp.bfloat16...  13.1 us
    sub x4, matrix products, attend(): powers = jnp.exp(scores - highest)  11.7 us
    unnamed x43, local copies, waits for them, and re-layouts  10.7 us
    all_to_all x1, starting transfers between devices, body(): lax.all_to_all(counts, ('sess', 'rep'), split_axis=0, concat_axis=0, tile...  6.33 us
    slice x2, local copies, waits for them, and re-layouts, attend(): prompts[:, :, KVH * HD:].reshape(session_total, PROMPT, KVH, HD)  5.48 us
  transfers between devices with their start and end apart: 6, of which 4 were waited for; matrix products, arithmetic and copies ran while one was open for 20% of the time, Pallas kernels for 0%

commit v1 on v0

--- a/solution.py
+++ b/solution.py
@@ -148,13 +148,19 @@
         .at[slot_place]
         .set(own_columns)
     )
-    arrived = lax.all_to_all(
-        buffer.reshape(owner_count, per_owner * slot_cap, own_columns.shape[1]),
-        ("sess", "rep"),
-        split_axis=0,
-        concat_axis=0,
-        tiled=True,
-    )
+    array = buffer.reshape(owner_count, per_owner * slot_cap, own_columns.shape[1])
+    ways, here = (lax.axis_size(("sess", "rep")), lax.axis_index(("sess", "rep")))
+    width = array.shape[0] // ways
+    shape = list(array.shape)
+    shape[0] = width
+    height = shape[0]
+    shape[0] = height * ways
+    arrived = jnp.zeros(shape, array.dtype)
+    for mask in range(ways):
+        part = lax.dynamic_slice_in_dim(array, (here ^ mask) * width, width, axis=0)
+        if mask:
+            part = lax.ppermute(part, ("sess", "rep"), [(d, d ^ mask) for d in range(ways)])
+        arrived = lax.dynamic_update_slice_in_dim(arrived, part, (here ^ mask) * height, axis=0)
     counts_in = lax.all_to_all(counts, ("sess", "rep"), split_axis=0, concat_axis=0, tiled=True)
     arrived_rows = arrived.reshape(owner_count, per_owner, slot_cap, arrived.shape[2])
     regrouped = lax.all_to_all(arrived_rows, "inner", split_axis=1, concat_axis=3, tiled=True)

time: 215 us -> 224 us (1.042)
  local copies, waits for them, and re-layouts: 52.8 us -> 77.1 us
  waiting for transfers between devices: 92.3 us -> 70.2 us
  starting transfers between devices: 19.5 us -> 25.4 us
    all_to_all x1 -> x0, waiting for transfers between devices: 24.4 us -> none  [body(): lax.all_to_all(buffer.reshape(owner_count, per_owner * slot_cap, own_colu...]
    dynamic_update_slice x0 -> x8, local copies, waits for them, and re-layouts: none -> 24 us  [body(): lax.dynamic_update_slice_in_dim(arrived, part, (here ^ mask) * height, ax...]
    ppermute x0 -> x7, starting transfers between devices: none -> 10.3 us  [body(): lax.ppermute(part, ('sess', 'rep'), [(d, d ^ mask) for d in range(ways)])]
    ppermute x0 -> x7, waiting for transfers between devices: none -> 6.69 us  [body(): lax.ppermute(part, ('sess', 'rep'), [(d, d ^ mask) for d in range(ways)])]
    all_to_all x1 -> x0, starting transfers between devices: 4.63 us -> none  [body(): lax.all_to_all(buffer.reshape(owner_count, per_owner * slot_cap, own_colu...]
    all_gather x1, waiting for transfers between devices: 33.9 us -> 30.4 us  [body(): piece = lax.all_gather(prompt_cache, 'sess', axis=0, tiled=True)]
    unnamed x43 -> x51, local copies, waits for them, and re-layouts: 10.7 us -> 11.8 us
  transfers between devices with their start and end apart: 6 -> 12, of which waited for: 4 -> 4; matrix products, arithmetic and copies ran while one was open for 20% -> 30% of each run, Pallas kernels for 0% -> 0%
where the time goes in v1:
time: 224 us; the launch traced here: 223 us
  local copies, waits for them, and re-layouts  77.1 us (34%)
  waiting for transfers between devices  70.2 us (31%)
  matrix products  28.5 us (13%)
  starting transfers between devices  25.4 us (11%)
  between operations  15.3 us (7%)
  other arithmetic  6.03 us (3%)
    all_gather x1, waiting for transfers between devices, body(): piece = lax.all_gather(prompt_cache, 'sess', axis=0, tiled=True)  30.4 us
    all_to_all x1, waiting for transfers between devices, body(): lax.all_to_all(chosen.astype(jnp.bfloat16), ('inner', 'rep'), split_axis=...  28.2 us
    dynamic_update_slice x8, local copies, waits for them, and re-layouts, body(): lax.dynamic_update_slice_in_dim(arrived, part, (here ^ mask) * height, ax...  24 us
    scatter x1, local copies, waits for them, and re-layouts, body(): compact = jnp.zeros((per_device, SLOTS, projected.shape[2]), jnp.bfloat16...  13.1 us
    unnamed x51, local copies, waits for them, and re-layouts  11.8 us
    sub x4, matrix products, attend(): powers = jnp.exp(scores - highest)  11.7 us
    ppermute x7, starting transfers between devices, body(): lax.ppermute(part, ('sess', 'rep'), [(d, d ^ mask) for d in range(ways)])  10.3 us
    ppermute x7, waiting for transfers between devices, body(): lax.ppermute(part, ('sess', 'rep'), [(d, d ^ mask) for d in range(ways)])  6.69 us
  transfers between devices with their start and end apart: 12, of which 4 were waited for; matrix products, arithmetic and copies ran while one was open for 30% of the time, Pallas kernels for 0%

profile of v1, /device:TPU:0, one launch (start us, length us, event | category | flops | bytes accessed | tf_op | source)
XLA Modules:
  0.0 222.6 jit_solution(16809155013802886784)
XLA Ops:
  7.4 1.9 copy-done
  9.3 3.4 %fusion.175 = f32[256,896]{0,1:T(8,128)} fusion(bf16[256,1792]{1,0:T(8,128)(2,1)} %param.11, bf16[1792,896]{1,0:T(8,128)(2,1)S(1)} %copy-done), kind=kOutput, calls=%fused_computation.197 | convolution fusion | flops 822083584 | bytes 5046272 | tf_op jit(solution)/shard_map/dot_general | solution.py:142
  14.4 6.3 %all-to-all-start = ((s32[8,1,4]{2,1,0:T(1,128)}), s32[8,1,4]{2,1,0:T(1,128)S(1)}, u32[]{:S(2)}, u32[]{:S(2)}) async-start(s32[8,1,4]{2,1,0:T(1,128)} %bitcast.1), calls=%async_computation | async-start | bytes 8192 | tf_op jit(solution)/shard_map/all_to_all | solution.py:164
  20.7 4.8 %copy.118 = bf16[896,1536]{0,1:T(8,128)(2,1)} copy(bf16[896,1536]{1,0:T(8,128)(2,1)} %param.18) | data formatting | bytes 5505024 | tf_op args[7]
  26.8 1.3 copy.129
  30.1 4.4 %reduce-scatter.2.cloned.1.call-done = f32[256,448]{0,1:T(8,128)} async-done(((f32[256,896]{0,1:T(8,128)}), f32[256,448]{0,1:T(8,128)}) %reduce-scatter.2.cloned.1.call-update) | async-done | bytes 458768 | tf_op jit(solution)/shard_map/reduce_scatter | solution.py:143
  34.5 1.0 convert_element_type.78
  35.7 1.6 scatter_custom_fusion
  37.6 1.6 collective-permute-start.1
  39.8 2.5 %collective-permute-start.3 = (bf16[1,48,448]{2,0,1:T(2,128)(2,1)S(1)}, bf16[1,48,448]{2,0,1:T(2,128)(2,1)S(1)}, u32[]{:S(2)}, u32[]{:S(2)}) collective-permute-start(bf16[1,48,448]{2,0,1:T(2,128)(2,1)S(1)} %copy.135), channel_id=1, source_target_pairs={{0,8},{1,9},{4,12},{5,13},{8,0},{9,1},{12,4},{13,5},{2,10},{3,11},... | collective-permute-start | bytes 129032 | tf_op jit(solution)/shard_map/ppermute | solution.py:162
  42.7 3.4 %collective-permute-start.5 = (bf16[1,48,448]{2,0,1:T(2,128)(2,1)S(1)}, bf16[1,48,448]{2,0,1:T(2,128)(2,1)S(1)}, u32[]{:S(2)}, u32[]{:S(2)}) collective-permute-start(bf16[1,48,448]{2,0,1:T(2,128)(2,1)S(1)} %copy.137), channel_id=1, source_target_pairs={{0,12},{1,13},{4,8},{5,9},{8,4},{9,5},{12,0},{13,1},{2,14},{3,15},... | collective-permute-start | bytes 129032 | tf_op jit(solution)/shard_map/ppermute | solution.py:162
  46.1 6.7 %collective-permute-done.1 = bf16[1,48,448]{2,0,1:T(2,128)(2,1)S(1)} collective-permute-done((bf16[1,48,448]{2,0,1:T(2,128)(2,1)S(1)}, bf16[1,48,448]{2,0,1:T(2,128)(2,1)S(1)}, u32[]{:S(2)}, u32[]{:S(2)}) %collective-permute-start.1) | collective-permute-done | bytes 43040 | tf_op jit(solution)/shard_map/ppermute | solution.py:162
  52.8 2.2 collective-permute-start.6
  55.9 0.8 broadcast_in_dim.60
  56.7 3.0 %dynamic_update_slice.24 = bf16[8,48,448]{2,0,1:T(8,128)(2,1)} dynamic-update-slice(bf16[8,48,448]{2,0,1:T(8,128)(2,1)} %broadcast_in_dim.60, bf16[1,48,448]{2,0,1:T(2,128)(2,1)S(1)} %copy.131, s32[]{:T(128)S(6)} %select_n.135, s32[]{:T(128)} %constant.97.clone.1, s32[]{:T(128)} %constant.97.clone.1) | dynamic-update-slice | bytes 86020 | tf_op jit(solution)/shard_map/dynamic_update_slice | solution.py:163
  59.7 3.0 %dynamic_update_slice.25 = bf16[8,48,448]{2,0,1:T(8,128)(2,1)} dynamic-update-slice(bf16[8,48,448]{2,0,1:T(8,128)(2,1)} %dynamic_update_slice.24, bf16[1,48,448]{2,0,1:T(2,128)(2,1)S(1)} %collective-permute-done, s32[]{:T(128)S(6)} %select_n.136, s32[]{:T(128)} %constant.97.clone.1, s32[]{:T(128)} %constant.97.clone.1) | dynamic-update-slice | bytes 86020 | tf_op jit(solution)/shard_map/dynamic_update_slice | solution.py:163
  62.7 3.0 %dynamic_update_slice.26 = bf16[8,48,448]{2,0,1:T(8,128)(2,1)} dynamic-update-slice(bf16[8,48,448]{2,0,1:T(8,128)(2,1)} %dynamic_update_slice.25, bf16[1,48,448]{2,0,1:T(2,128)(2,1)S(1)} %collective-permute-done.1, s32[]{:T(128)S(6)} %select_n.137, s32[]{:T(128)} %constant.97.clone.1, s32[]{:T(128)} %constant.97.clone.1) | dynamic-update-slice | bytes 86020 | tf_op jit(solution)/shard_map/dynamic_update_slice | solution.py:163
  65.7 3.0 %dynamic_update_slice.27 = bf16[8,48,448]{2,0,1:T(8,128)(2,1)} dynamic-update-slice(bf16[8,48,448]{2,0,1:T(8,128)(2,1)} %dynamic_update_slice.26, bf16[1,48,448]{2,0,1:T(2,128)(2,1)S(1)} %collective-permute-done.2, s32[]{:T(128)S(6)} %select_n.138, s32[]{:T(128)} %constant.97.clone.1, s32[]{:T(128)} %constant.97.clone.1) | dynamic-update-slice | bytes 86020 | tf_op jit(solution)/shard_map/dynamic_update_slice | solution.py:163
  68.7 3.0 %dynamic_update_slice.28 = bf16[8,48,448]{2,0,1:T(8,128)(2,1)} dynamic-update-slice(bf16[8,48,448]{2,0,1:T(8,128)(2,1)} %dynamic_update_slice.27, bf16[1,48,448]{2,0,1:T(2,128)(2,1)S(1)} %collective-permute-done.3, s32[]{:T(128)S(6)} %select_n.139, s32[]{:T(128)} %constant.97.clone.1, s32[]{:T(128)} %constant.97.clone.1) | dynamic-update-slice | bytes 86020 | tf_op jit(solution)/shard_map/dynamic_update_slice | solution.py:163
  71.7 3.0 %dynamic_update_slice.29 = bf16[8,48,448]{2,0,1:T(8,128)(2,1)} dynamic-update-slice(bf16[8,48,448]{2,0,1:T(8,128)(2,1)} %dynamic_update_slice.28, bf16[1,48,448]{2,0,1:T(2,128)(2,1)S(1)} %collective-permute-done.4, s32[]{:T(128)S(6)} %select_n.140, s32[]{:T(128)} %constant.97.clone.1, s32[]{:T(128)} %constant.97.clone.1) | dynamic-update-slice | bytes 86020 | tf_op jit(solution)/shard_map/dynamic_update_slice | solution.py:163
  74.7 3.0 %dynamic_update_slice.30 = bf16[8,48,448]{2,0,1:T(8,128)(2,1)} dynamic-update-slice(bf16[8,48,448]{2,0,1:T(8,128)(2,1)} %dynamic_update_slice.29, bf16[1,48,448]{2,0,1:T(2,128)(2,1)S(1)} %collective-permute-done.5, s32[]{:T(128)S(6)} %select_n.141, s32[]{:T(128)} %constant.97.clone.1, s32[]{:T(128)} %constant.97.clone.1) | dynamic-update-slice | bytes 86020 | tf_op jit(solution)/shard_map/dynamic_update_slice | solution.py:163
  77.7 3.0 %dynamic_update_slice.31 = bf16[8,48,448]{2,0,1:T(8,128)(2,1)} dynamic-update-slice(bf16[8,48,448]{2,0,1:T(8,128)(2,1)} %dynamic_update_slice.30, bf16[1,48,448]{2,0,1:T(2,128)(2,1)S(1)} %collective-permute-done.6, s32[]{:T(128)S(6)} %select_n.142, s32[]{:T(128)} %constant.97.clone.1, s32[]{:T(128)} %constant.97.clone.1) | dynamic-update-slice | bytes 86020 | tf_op jit(solution)/shard_map/dynamic_update_slice | solution.py:163
  80.6 3.6 %all-to-all-start.1 = ((bf16[8,4,12,448]{3,0,2,1:T(8,128)(2,1)}), bf16[8,4,12,448]{3,0,2,1:T(8,128)(2,1)S(1)}, u32[]{:S(2)}, u32[]{:S(2)}) async-start(bf16[8,4,12,448]{3,0,2,1:T(8,128)(2,1)} %bitcast.9), calls=%async_computation.2 | async-start | bytes 786432 | tf_op jit(solution)/shard_map/all_to_all | solution.py:166
  84.3 30.4 %all-gather.2.cloned.1.call-done = bf16[8,256,1024]{2,1,0:T(8,128)(2,1)} async-done(((bf16[2,256,1024]{2,1,0:T(8,128)(2,1)}), bf16[8,256,1024]{2,1,0:T(8,128)(2,1)}) %all-gather.2.cloned.1.call-update) | async-done | bytes 4194320 | tf_op jit(solution)/shard_map/all_gather | solution.py:192
  114.7 4.7 %fusion.22 = bf16[8,256,1024]{2,0,1:T(8,128)(2,1)S(1)} fusion(bf16[8,256,1024]{2,1,0:T(8,128)(2,1)} %all-gather.2.cloned.1.call-done, s32[8]{0:T(128)S(1)} %select_reduce_fusion), kind=kOutput, calls=%fused_computation.34 | convolution fusion | flops 35651648 | bytes 8388640 | tf_op jit(solution)/shard_map/sp,ptc->stc/dot_general | solution.py:194
  119.4 4.3 %copy.108 = bf16[8,256,1024]{2,1,0:T(8,128)(2,1)} copy(bf16[8,256,1024]{2,0,1:T(8,128)(2,1)S(1)} %fusion.22) | data formatting | bytes 8388608 | tf_op jit(solution)/shard_map/convert_element_type | solution.py:196
  123.7 5.1 %all-to-all-start.2 = ((bf16[8,256,1024]{2,1,0:T(8,128)(2,1)}), bf16[8,256,1024]{2,1,0:T(8,128)(2,1)}, u32[]{:S(2)}, u32[]{:S(2)}) async-start(bf16[8,256,1024]{2,1,0:T(8,128)(2,1)} %copy.108), calls=%async_computation.3 | async-start | bytes 8388608 | tf_op jit(solution)/shard_map/all_to_all | solution.py:195
  128.8 0.8 and_or_fusion
  130.6 13.1 %scatter_fusion = bf16[2,96,896]{2,1,0:T(8,128)(2,1)S(1)} fusion(bf16[2,96,896]{2,1,0:T(8,128)(2,1)S(1)} %broadcast_in_dim.57, s32[192]{0:T(256)S(1)} %reshape.305, bf16[192,896]{1,0:T(8,128)(2,1)S(1)} %reshape.307), kind=kCustom, calls=%fused_computation.1 | custom fusion | bytes 1033728 | tf_op jit(solution)/shard_map/scatter | solution.py:181
  144.5 0.9 fusion.68
  145.4 1.2 convolution_convert_fusion
  146.5 1.1 fusion.113
  148.6 28.2 %all-to-all-done.2 = bf16[8,256,1024]{2,1,0:T(8,128)(2,1)} async-done(((bf16[8,256,1024]{2,1,0:T(8,128)(2,1)}), bf16[8,256,1024]{2,1,0:T(8,128)(2,1)}, u32[]{:S(2)}, u32[]{:S(2)}) %all-to-all-start.2) | async-done | bytes 4194336 | tf_op jit(solution)/shard_map/all_to_all | solution.py:195
  176.8 2.6 %copy.109 = bf16[2,4,256,1024]{3,2,1,0:T(8,128)(2,1)S(1)} copy(bf16[2,4,256,1024]{3,2,0,1:T(8,128)(2,1)} %bitcast.16) | data formatting | bytes 8388608 | tf_op jit(solution)/shard_map/all_to_all | solution.py:195
  179.4 2.5 %fusion.154 = (bf16[2,1024,512]{2,1,0:T(8,128)(2,1)}, bf16[2,1024,512]{2,1,0:T(8,128)(2,1)}) fusion(bf16[2,1024,1024]{2,1,0:T(8,128)(2,1)S(1)} %bitcast.185), kind=kLoop, calls=%fused_computation.192 | loop fusion | bytes 8388608 | tf_op jit(solution)/shard_map/slice | solution.py:61
  181.8 3.0 %copy.114 = bf16[2,1024,512]{1,2,0:T(8,128)(2,1)S(1)} copy(bf16[2,1024,512]{2,1,0:T(8,128)(2,1)} %get-tuple-element.10) | data formatting | bytes 4194304 | tf_op jit(solution)/shard_map/slice | solution.py:60
  184.9 2.6 %copy.116 = bf16[2,1024,4,128]{3,1,0,2:T(8,128)(2,1)} copy(bf16[2,1024,4,128]{1,3,2,0:T(8,128)(2,1)S(1)} %bitcast.187) | data formatting | bytes 4194304 | tf_op jit(solution)/shard_map/reshape | solution.py:60
  187.5 3.8 %fusion.155 = (f32[2,3,96]{2,1,0:T(4,128)S(1)}, f32[2,3,96,1120]{3,2,1,0:T(8,128)}) fusion(pred[2,96,1120]{2,1,0:T(8,128)(4,1)S(1)} %copy-done.9, bf16[2,1024,4,128]{3,1,0,2:T(8,128)(2,1)} %copy.116, bf16[2,96,12,128]{3,1,2,0:T(8,128)(2,1)S(1)} %fusion.32, bf16[2,96,4,128]{3,1,2,0:T(8,128)(2,1)S(1)} %copy-done.10), kind=kOutput, calls=%fused_computation.193 | convolution fusion | flops 168879200 | bytes 5245184 | tf_op jit(solution)/shard_map/sub | solution.py:81
  191.3 2.6 %fusion.160 = (f32[2,3,96]{2,1,0:T(4,128)S(1)}, f32[2,3,96,1120]{3,2,1,0:T(8,128)}) fusion(pred[2,96,1120]{2,1,0:T(8,128)(4,1)S(1)} %copy-done.9, bf16[2,1024,4,128]{3,1,0,2:T(8,128)(2,1)S(1)} %copy-done.4, bf16[2,96,12,128]{3,1,2,0:T(8,128)(2,1)S(1)} %fusion.32, bf16[2,96,4,128]{3,1,2,0:T(8,128)(2,1)S(1)} %copy-done.10), kind=kOutput, calls=%fused_computation.194 | convolution fusion | flops 168879200 | bytes 5245184 | tf_op jit(solution)/shard_map/sub | solution.py:81
  193.9 2.6 %fusion.165 = (f32[2,3,96]{2,1,0:T(4,128)S(1)}, f32[2,3,96,1120]{3,2,1,0:T(8,128)}) fusion(pred[2,96,1120]{2,1,0:T(8,128)(4,1)S(1)} %copy-done.9, bf16[2,1024,4,128]{3,1,0,2:T(8,128)(2,1)S(1)} %copy-done.4, bf16[2,96,12,128]{3,1,2,0:T(8,128)(2,1)S(1)} %fusion.32, bf16[2,96,4,128]{3,1,2,0:T(8,128)(2,1)S(1)} %copy-done.10), kind=kOutput, calls=%fused_computation.195 | convolution fusion | flops 168879200 | bytes 5245184 | tf_op jit(solution)/shard_map/sub | solution.py:81
  196.5 2.7 %fusion.170 = (f32[2,3,96]{2,1,0:T(4,128)S(1)}, f32[2,3,96,1120]{3,2,1,0:T(8,128)}) fusion(pred[2,96,1120]{2,1,0:T(8,128)(4,1)S(1)} %copy-done.9, bf16[2,1024,4,128]{3,1,0,2:T(8,128)(2,1)S(1)} %copy-done.4, bf16[2,96,12,128]{3,1,2,0:T(8,128)(2,1)S(1)} %fusion.32, bf16[2,96,4,128]{3,1,2,0:T(8,128)(2,1)S(1)} %copy-done.10), kind=kOutput, calls=%fused_computation.196 | convolution fusion | flops 168879200 | bytes 5245184 | tf_op jit(solution)/shard_map/sub | solution.py:81
  199.2 3.0 %copy.110 = bf16[2,1024,512]{1,2,0:T(8,128)(2,1)S(1)} copy(bf16[2,1024,512]{2,1,0:T(8,128)(2,1)} %get-tuple-element.9) | data formatting | bytes 4194304 | tf_op jit(solution)/shard_map/slice | solution.py:61
  202.2 2.8 %copy.112 = bf16[2,1024,4,128]{3,1,0,2:T(8,128)(2,1)} copy(bf16[2,1024,4,128]{1,3,2,0:T(8,128)(2,1)S(1)} %bitcast.188) | data formatting | bytes 4194304 | tf_op jit(solution)/shard_map/reshape | solution.py:61
  205.0 2.6 %fusion.40 = bf16[2,96,3,128]{3,1,2,0:T(8,128)(2,1)S(1)} fusion(f32[2,3,96,1120]{3,2,1,0:T(8,128)} %get-tuple-element.26, f32[2,3,96]{2,1,0:T(4,128)S(1)} %get-tuple-element.25, bf16[2,1024,4,128]{3,1,0,2:T(8,128)(2,1)} %copy.112, bf16[2,96,4,128]{3,1,2,0:T(8,128)(2,1)S(1)} %copy-done.17), kind=kOutput, calls=%fused_computation.64 | convolution fusion | flops 167661568 | bytes 5024000 | tf_op jit(solution)/shard_map/chqk,ckd->cqhd/dot_general | solution.py:84
  209.0 1.2 copy-done.19
  210.7 1.2 copy-done.18
  212.8 0.8 copy-done.13
  213.6 1.5 fusion.30
  (109 shorter events, 12.6 us)
Async XLA Ops:
  7.4 1.9 copy-start
  7.4 6.0 %copy-start.11 = (s32[256,1]{0,1:T(1,128)S(1)}, s32[256,1]{0,1:T(1,128)}, u32[]{:S(2)}) copy-start(s32[256,1]{0,1:T(1,128)} %param.12) | copy-start | bytes 3076
  7.4 27.1 %reduce-scatter.2.cloned.1.call-start = ((), (), s32[]{:S(2)}) async-start(), calls=%async_computation.4 | async-start | bytes 1376256 | tf_op jit(solution)/shard_map/reduce_scatter | solution.py:143
  12.7 101.9 %all-gather.2.cloned.1.call-start = ((), (), s32[]{:S(2)}) async-start(), calls=%async_computation.5 | async-start | bytes 5242880 | tf_op jit(solution)/shard_map/all_gather | solution.py:192
  14.4 15.0 %all-to-all-start = ((s32[8,1,4]{2,1,0:T(1,128)}), s32[8,1,4]{2,1,0:T(1,128)S(1)}, u32[]{:S(2)}, u32[]{:S(2)}) async-start(s32[8,1,4]{2,1,0:T(1,128)} %bitcast.1), calls=%async_computation | async-start | bytes 8192 | tf_op jit(solution)/shard_map/all_to_all | solution.py:164
  20.7 4.9 %copy-start.12 = (bf16[896]{0:T(1024)(128)(2,1)S(1)}, bf16[896]{0:T(1024)(128)(2,1)}, u32[]{:S(2)}) copy-start(bf16[896]{0:T(1024)(128)(2,1)} %param.17) | copy-start | bytes 5380
  20.7 4.9 %copy-start.5 = (bf16[896,512]{1,0:T(8,128)(2,1)S(1)}, bf16[896,512]{1,0:T(8,128)(2,1)}, u32[]{:S(2)}) copy-start(bf16[896,512]{1,0:T(8,128)(2,1)} %param.19) | copy-start | bytes 2752516
  25.5 1.2 copy-start.6
  25.5 2.5 %copy-start.14 = (s32[32]{0:T(128)S(1)}, s32[32]{0:T(128)}, u32[]{:S(2)}) copy-start(s32[32]{0:T(128)} %param.13) | copy-start | bytes 388
  25.5 2.6 %copy-start.15 = (s32[8]{0:T(128)S(1)}, s32[8]{0:T(128)}, u32[]{:S(2)}) copy-start(s32[8]{0:T(128)} %param.14) | copy-start | bytes 100
  37.5 5.2 %collective-permute-start = (bf16[1,48,448]{2,0,1:T(2,128)(2,1)S(1)}, bf16[1,48,448]{2,0,1:T(2,128)(2,1)S(1)}, u32[]{:S(2)}, u32[]{:S(2)}) collective-permute-start(bf16[1,48,448]{2,0,1:T(2,128)(2,1)S(1)} %copy.132), channel_id=1, source_target_pairs={{0,1},{1,0},{4,5},{5,4},{8,9},{9,8},{12,13},{13,12},{2,3},{3,2},{6... | collective-permute-start | bytes 129032 | tf_op jit(solution)/shard_map/ppermute | solution.py:162
  37.6 15.2 %collective-permute-start.1 = (bf16[1,48,448]{2,0,1:T(2,128)(2,1)S(1)}, bf16[1,48,448]{2,0,1:T(2,128)(2,1)S(1)}, u32[]{:S(2)}, u32[]{:S(2)}) collective-permute-start(bf16[1,48,448]{2,0,1:T(2,128)(2,1)S(1)} %copy.133), channel_id=1, source_target_pairs={{0,4},{1,5},{4,0},{5,1},{8,12},{9,13},{12,8},{13,9},{2,6},{3,7},{6... | collective-permute-start | bytes 129032 | tf_op jit(solution)/shard_map/ppermute | solution.py:162
  39.3 26.4 %collective-permute-start.2 = (bf16[1,48,448]{2,0,1:T(2,128)(2,1)S(1)}, bf16[1,48,448]{2,0,1:T(2,128)(2,1)S(1)}, u32[]{:S(2)}, u32[]{:S(2)}) collective-permute-start(bf16[1,48,448]{2,0,1:T(2,128)(2,1)S(1)} %copy.134), channel_id=1, source_target_pairs={{0,5},{1,4},{4,1},{5,0},{8,13},{9,12},{12,9},{13,8},{2,7},{3,6},{6... | collective-permute-start | bytes 129032 | tf_op jit(solution)/shard_map/ppermute | solution.py:162
  39.8 28.9 %collective-permute-start.3 = (bf16[1,48,448]{2,0,1:T(2,128)(2,1)S(1)}, bf16[1,48,448]{2,0,1:T(2,128)(2,1)S(1)}, u32[]{:S(2)}, u32[]{:S(2)}) collective-permute-start(bf16[1,48,448]{2,0,1:T(2,128)(2,1)S(1)} %copy.135), channel_id=1, source_target_pairs={{0,8},{1,9},{4,12},{5,13},{8,0},{9,1},{12,4},{13,5},{2,10},{3,11},... | collective-permute-start | bytes 129032 | tf_op jit(solution)/shard_map/ppermute | solution.py:162
  42.3 29.3 %collective-permute-start.4 = (bf16[1,48,448]{2,0,1:T(2,128)(2,1)S(1)}, bf16[1,48,448]{2,0,1:T(2,128)(2,1)S(1)}, u32[]{:S(2)}, u32[]{:S(2)}) collective-permute-start(bf16[1,48,448]{2,0,1:T(2,128)(2,1)S(1)} %copy.136), channel_id=1, source_target_pairs={{0,9},{1,8},{4,13},{5,12},{8,1},{9,0},{12,5},{13,4},{2,11},{3,10},... | collective-permute-start | bytes 129032 | tf_op jit(solution)/shard_map/ppermute | solution.py:162
  42.7 31.9 %collective-permute-start.5 = (bf16[1,48,448]{2,0,1:T(2,128)(2,1)S(1)}, bf16[1,48,448]{2,0,1:T(2,128)(2,1)S(1)}, u32[]{:S(2)}, u32[]{:S(2)}) collective-permute-start(bf16[1,48,448]{2,0,1:T(2,128)(2,1)S(1)} %copy.137), channel_id=1, source_target_pairs={{0,12},{1,13},{4,8},{5,9},{8,4},{9,5},{12,0},{13,1},{2,14},{3,15},... | collective-permute-start | bytes 129032 | tf_op jit(solution)/shard_map/ppermute | solution.py:162
  52.8 24.9 %collective-permute-start.6 = (bf16[1,48,448]{2,0,1:T(2,128)(2,1)S(1)}, bf16[1,48,448]{2,0,1:T(2,128)(2,1)S(1)}, u32[]{:S(2)}, u32[]{:S(2)}) collective-permute-start(bf16[1,48,448]{2,0,1:T(2,128)(2,1)S(1)} %copy.138), channel_id=1, source_target_pairs={{0,13},{1,12},{4,9},{5,8},{8,5},{9,4},{12,1},{13,0},{2,15},{3,14},... | collective-permute-start | bytes 129032 | tf_op jit(solution)/shard_map/ppermute | solution.py:162
  80.6 43.0 %all-to-all-start.1 = ((bf16[8,4,12,448]{3,0,2,1:T(8,128)(2,1)}), bf16[8,4,12,448]{3,0,2,1:T(8,128)(2,1)S(1)}, u32[]{:S(2)}, u32[]{:S(2)}) async-start(bf16[8,4,12,448]{3,0,2,1:T(8,128)(2,1)} %bitcast.9), calls=%async_computation.2 | async-start | bytes 786432 | tf_op jit(solution)/shard_map/all_to_all | solution.py:166
  123.7 53.1 %all-to-all-start.2 = ((bf16[8,256,1024]{2,1,0:T(8,128)(2,1)}), bf16[8,256,1024]{2,1,0:T(8,128)(2,1)}, u32[]{:S(2)}, u32[]{:S(2)}) async-start(bf16[8,256,1024]{2,1,0:T(8,128)(2,1)} %copy.108), calls=%async_computation.3 | async-start | bytes 8388608 | tf_op jit(solution)/shard_map/all_to_all | solution.py:195
  143.6 0.9 copy-start.8
  143.8 1.6 copy-start.7
  144.3 2.2 %copy-start.2 = (bf16[896,1536]{0,1:T(8,128)(2,1)S(1)}, bf16[896,1536]{0,1:T(8,128)(2,1)}, u32[]{:S(2)}) copy-start(bf16[896,1536]{0,1:T(8,128)(2,1)} %copy.118) | copy-start | bytes 8257540
  184.8 2.6 %copy-start.9 = (pred[2,96,1120]{2,1,0:T(8,128)(4,1)S(1)}, pred[2,96,1120]{2,1,0:T(8,128)(4,1)}, u32[]{:S(2)}) copy-start(pred[2,96,1120]{2,1,0:T(8,128)(4,1)} %and_or_fusion) | copy-start | bytes 645124
  184.9 2.6 %copy-start.10 = (bf16[2,96,4,128]{3,1,2,0:T(8,128)(2,1)S(1)}, bf16[2,96,4,128]{3,1,2,0:T(8,128)(2,1)}, u32[]{:S(2)}) copy-start(bf16[2,96,4,128]{3,1,2,0:T(8,128)(2,1)} %fusion.68) | copy-start | bytes 589828
  187.5 3.8 %copy-start.4 = (bf16[2,1024,4,128]{3,1,0,2:T(8,128)(2,1)S(1)}, bf16[2,1024,4,128]{3,1,0,2:T(8,128)(2,1)}, u32[]{:S(2)}) copy-start(bf16[2,1024,4,128]{3,1,0,2:T(8,128)(2,1)} %copy.116) | copy-start | bytes 6291460
  202.2 2.9 %copy-start.17 = (bf16[2,96,4,128]{3,1,2,0:T(8,128)(2,1)S(1)}, bf16[2,96,4,128]{3,1,2,0:T(8,128)(2,1)}, u32[]{:S(2)}) copy-start(bf16[2,96,4,128]{3,1,2,0:T(8,128)(2,1)} %convolution_convert_fusion) | copy-start | bytes 589828
  205.0 2.6 %copy-start.3 = (bf16[2,1024,4,128]{3,1,0,2:T(8,128)(2,1)S(1)}, bf16[2,1024,4,128]{3,1,0,2:T(8,128)(2,1)}, u32[]{:S(2)}) copy-start(bf16[2,1024,4,128]{3,1,0,2:T(8,128)(2,1)} %copy.112) | copy-start | bytes 6291460
  205.0 3.3 %copy-start.20 = (f32[2,3,96,1120]{3,2,1,0:T(8,128)S(1)}, f32[2,3,96,1120]{3,2,1,0:T(8,128)}, u32[]{:S(2)}) copy-start(f32[2,3,96,1120]{3,2,1,0:T(8,128)} %get-tuple-element.28) | copy-start | bytes 7741444
  208.4 1.7 copy-start.19
  210.1 1.7 copy-start.18
  211.9 1.8 copy-start.13
  212.5 1.2 copy-start.16
  212.8 2.4 %copy-start.1 = (bf16[1792,896]{1,0:T(8,128)(2,1)S(1)}, bf16[1792,896]{1,0:T(8,128)(2,1)}, u32[]{:S(2)}) copy-start(bf16[1792,896]{1,0:T(8,128)(2,1)} %param.16) | copy-start | bytes 9633796
Sparse Core Ops, SparseCore 0:
  12.9 21.5 reduce-scatter.1
Sparse Core Ops, SparseCore 1:
  14.8 99.8 all-gather.1
